TPU v7x, 128 devices: a whole 4x4x4 slice. The times are simulated.
128 devices in a mesh: dp: 4 (over z), expert: 32 (over x, y, core).
Axes of the slice: x: 4, y: 4, z: 4, core: 2. Of those that a mesh axis runs over, the one named last changes fastest.
Arguments:
- tokens: bfloat16 [4, 8192, 2048], P('dp', 'expert'), may hold values from -8 to 8
- cotangent: bfloat16 [4, 8192, 2048], P('dp', 'expert'), may hold values from -8 to 8
- slot_rows: int32 [4, 32, 32, 32], P('dp', 'expert'), may hold values from 0 to 255, as said below
- slot_count: int32 [4, 32, 32], P('dp', 'expert'), may hold values from 8 to 32, as said below
- slot_weight: float32 [4, 32, 32, 32], P('dp', 'expert'), may hold values from 0.1 to 1
- w_in: bfloat16 [32, 2, 2048, 512], P('expert'), may hold values from -5 to 5
- w_out: bfloat16 [32, 512, 2048], P('expert'), may hold values from -5 to 5
- momentum_in: float32 [32, 2, 2048, 512], P('expert', None, 'dp'), may hold values from -6 to 6
- momentum_out: float32 [32, 512, 2048], P('expert', None, 'dp'), may hold values from -6 to 6
Outputs:
- token_grad: bfloat16 [4, 8192, 2048], P('dp', 'expert')
- w_in_new: bfloat16 [32, 2, 2048, 512], P('expert')
- w_out_new: bfloat16 [32, 512, 2048], P('expert')
- momentum_in_new: float32 [32, 2, 2048, 512], P('expert', None, 'dp')
- momentum_out_new: float32 [32, 512, 2048], P('expert', None, 'dp')
Inputs may be any that keep to these rules, and one draw needn't show every extreme that they name: `slot_rows`: entries index the source's 256 tokens; the 32 entries of one source and expert are distinct. Slots c < slot_count are used. In every replica some expert receives 32 rows from every source.
All inputs are finite; a program needn't handle non-finite values.
Results may differ from a plain program's by a relative error of at most 0.0064.
Values may be sent and summed in bfloat16 or wider, within the bound.
A program may use at most 128 MiB of HBM per device.

v0:
```python
import jax
import jax.numpy as jnp
from jax import lax
from jax.experimental import pallas as pl
from jax.experimental.pallas import tpu as pltpu
from jax.sharding import PartitionSpec as P

EPS = 1e-06
MOMENTUM = 0.9
RATE = 0.1
MESH = pl.DeviceIdType.MESH

D = 2048
FF = 512
HALF = 1024
QUARTER = 512
CAP = 32
STAGES_X = 2
STAGES_G = 4
STAGES_R = 2
ROWS = 1024
BF16 = jnp.bfloat16
F32 = jnp.float32


def dot(a, b, ca, cb):
    return lax.dot_general(a, b, (((ca,), (cb,)), ((), ())), preferred_element_type=F32)


def kernel(
    tok_h, cot_h, rows_v, count_v, weight_v, win_h, wout_h, min_h, mout_h,
    tg_h, nwin_h, nwout_h, nmin_h, nmout_h,
    tok, cot, onehot, scale, send_x, send_g, mid_x, mid_g, xs, gs_, win, wout,
    act_a, act_s, hid, dh, dgu, grad_s, grad_r, mom_in, mom_out, gram,
    load_sem, p1_send, p1_recv, p2_send, p2_recv, self1, self2,
    rs_send, rs_recv, rs_self, gram_send, gram_recv, ag_send, ag_recv, fw_send, fw_recv, out_sem,
):
    z = lax.axis_index("dp")
    e = lax.axis_index("expert")
    x = e // 8
    y = lax.rem(e // 2, 4)
    c = lax.rem(e, 2)
    scale_in = D ** (-0.5)
    scale_out = FF ** (-0.5)

    def expert_id(px, py, pc):
        return (px * 4 + py) * 2 + pc

    loads = [
        (tok_h, tok), (cot_h, cot), (win_h, win), (wout_h, wout), (min_h, mom_in), (mout_h, mom_out),
    ]
    load = [pltpu.make_async_copy(s, d, load_sem.at[i]) for i, (s, d) in enumerate(loads)]
    for copy in load:
        copy.start()

    barrier = pltpu.get_barrier_semaphore()

    def greet(device):
        pl.semaphore_signal(barrier, inc=1, device_id=device, device_id_type=MESH)

    for k in range(1, 8):
        greet((z, expert_id(lax.rem(x + k // 2, 4), y, lax.rem(c + k % 2, 2))))
    for k in range(2, 8):
        greet((z, expert_id(x, lax.rem(y + k // 2, 4), lax.rem(c + k % 2, 2))))
    for k in range(1, 4):
        greet((lax.rem(z + k, 4), e))

    rows_t = rows_v[...]
    weight_t = weight_v[...]
    valid = lax.broadcasted_iota(jnp.int32, (CAP, 32), 0) < count_v[...]
    scale_t = jnp.where(valid, weight_t, 0.0)
    lane = lax.broadcasted_iota(jnp.int32, (CAP, 256), 1)
    for k in range(32):
        onehot[k * CAP : (k + 1) * CAP, :] = (lane == rows_t[:, k : k + 1]).astype(F32).astype(BF16)
        scale[k * CAP : (k + 1) * CAP, :] = jnp.broadcast_to(scale_t[:, k : k + 1], (CAP, 128))

    def gather(src, dst, c0, w, scaled):
        def step(m, _):
            r0 = pl.multiple_of(m * 256, 256)
            hot = onehot[pl.ds(r0, 256), :]
            for half in range(2):
                col = half * HALF + c0
                v = dot(hot, src[:, col : col + w], 1, 0)
                if scaled:
                    v = v * scale[pl.ds(r0, 256), 0:1]
                dst[m, :, :, :, col : col + w] = v.astype(BF16).reshape(4, 2, CAP, w)
            return 0

        lax.fori_loop(0, 4, step, 0)

    def p1_copy(send, mid, st, c0, w, half, k):
        pc = lax.rem(c + lax.rem(k, 2), 2)
        col = pl.ds(half * HALF + c0, w)
        mcol = pl.ds(c0, w)
        if half == 0:
            pa = lax.rem(x + k // 2, 4)
            peer = expert_id(pa, y, pc)
            src = send.at[pa, :, pc, :, col]
            dst = mid.at[0, :, x, c, :, mcol]
        else:
            pa = lax.rem(y + k // 2, 4)
            peer = expert_id(x, pa, pc)
            src = send.at[:, pa, pc, :, col]
            dst = mid.at[1, :, y, c, :, mcol]
        return pltpu.make_async_remote_copy(
            src_ref=src, dst_ref=dst, send_sem=p1_send.at[st, half, k], recv_sem=p1_recv.at[st, half, k],
            device_id=(z, peer), device_id_type=MESH,
        )

    def p1_self(send, mid, st, c0, w, half):
        col = pl.ds(half * HALF + c0, w)
        mcol = pl.ds(c0, w)
        if half == 0:
            return pltpu.make_async_copy(
                send.at[x, :, c, :, col], mid.at[0, :, x, c, :, mcol], self1.at[st, half]
            )
        return pltpu.make_async_copy(
            send.at[:, y, c, :, col], mid.at[1, :, y, c, :, mcol], self1.at[st, half]
        )

    def p2_copy(mid, fin, st, c0, w, half, k):
        col = pl.ds(half * HALF + c0, w)
        mcol = pl.ds(c0, w)
        if half == 0:
            pa = lax.rem(y + k, 4)
            peer = expert_id(x, pa, c)
            src = mid.at[0, pa, :, :, :, mcol]
            dst = fin.at[:, y, :, :, col]
        else:
            pa = lax.rem(x + k, 4)
            peer = expert_id(pa, y, c)
            src = mid.at[1, pa, :, :, :, mcol]
            dst = fin.at[x, :, :, :, col]
        return pltpu.make_async_remote_copy(
            src_ref=src, dst_ref=dst, send_sem=p2_send.at[st, half, k], recv_sem=p2_recv.at[st, half, k],
            device_id=(z, peer), device_id_type=MESH,
        )

    def p2_self(mid, fin, st, c0, w, half):
        col = pl.ds(half * HALF + c0, w)
        mcol = pl.ds(c0, w)
        if half == 0:
            return pltpu.make_async_copy(
                mid.at[0, y, :, :, :, mcol], fin.at[:, y, :, :, col], self2.at[st, half]
            )
        return pltpu.make_async_copy(
            mid.at[1, x, :, :, :, mcol], fin.at[x, :, :, :, col], self2.at[st, half]
        )

    def each(lo, hi, fn):
        def step(k, _):
            fn(k)
            return 0

        lax.fori_loop(lo, hi, step, 0)

    def start_first(args):
        send, mid, fin, st, c0, w = args

        def go(k):
            p1_copy(send, mid, st, c0, w, 0, k).start()
            p1_copy(send, mid, st, c0, w, 1, k).start()

        each(1, 8, go)
        for half in range(2):
            p1_self(send, mid, st, c0, w, half).start()

    def forward(args):
        send, mid, fin, st, c0, w = args
        for half in range(2):
            each(1, 8, lambda k: p1_copy(send, mid, st, c0, w, half, k).wait())
            p1_self(send, mid, st, c0, w, half).wait()
            each(1, 4, lambda k: p2_copy(mid, fin, st, c0, w, half, k).start())
            p2_self(mid, fin, st, c0, w, half).start()

    def arrive(args):
        send, mid, fin, st, c0, w = args
        for half in range(2):
            each(1, 4, lambda k: p2_copy(mid, fin, st, c0, w, half, k).wait())
            p2_self(mid, fin, st, c0, w, half).wait()

    wx, wg, wr = HALF // STAGES_X, HALF // STAGES_G, HALF // STAGES_R
    ex = [(send_x, mid_x, xs, s, s * wx, wx) for s in range(STAGES_X)]
    eg = [(send_g, mid_g, gs_, STAGES_X + s, s * wg, wg) for s in range(STAGES_G)]
    er = [(send_x, mid_x, send_g, STAGES_X + STAGES_G + s, s * wr, wr) for s in range(STAGES_R)]

    def activate(m):
        rows = xs[m].reshape(256, D)
        r = pl.ds(pl.multiple_of(m * 256, 256), 256)
        gate = dot(rows, win[0], 1, 0) * scale_in
        up = dot(rows, win[1], 1, 0) * scale_in
        sig = jax.nn.sigmoid(gate)
        act = gate * sig
        hid[r, :] = (act * up).astype(BF16)
        act_a[r, :] = up * sig * (1.0 + gate * (1.0 - sig))
        act_s[r, :] = act

    def out_copy(s, half):
        col = half * HALF + s * wg
        q, off = col // QUARTER, col % QUARTER
        return q, pltpu.make_async_remote_copy(
            src_ref=grad_s.at[2, q, :, pl.ds(off, wg)],
            dst_ref=grad_r.at[z, 2, :, pl.ds(off, wg)],
            send_sem=rs_send.at[2, s, half],
            recv_sem=rs_recv.at[2 + off // wg, lax.rem(q - z + 4, 4)],
            device_id=(q, e), device_id_type=MESH,
        ), pltpu.make_async_copy(
            grad_s.at[2, q, :, pl.ds(off, wg)], grad_r.at[z, 2, :, pl.ds(off, wg)], rs_self.at[2, s, half]
        )

    def grad_out(s):
        for half in range(2):
            col = half * HALF + s * wg
            q, off = col // QUARTER, col % QUARTER
            rows = gs_[:, :, :, :, col : col + wg].reshape(ROWS, wg)
            grad_s[2, q, :, off : off + wg] = (dot(hid[...], rows, 0, 0) * scale_out).astype(BF16)
            q, remote, local = out_copy(s, half)

            @pl.when(z != q)
            def _():
                remote.start()

            @pl.when(z == q)
            def _():
                local.start()

    def hidden_grad(s):
        def step(m, _):
            r = pl.ds(pl.multiple_of(m * 256, 256), 256)
            acc = None
            for half in range(2):
                col = half * HALF + s * wg
                rows = gs_[m, :, :, :, col : col + wg].reshape(256, wg)
                part = dot(rows, wout[:, col : col + wg], 1, 1)
                acc = part if acc is None else acc + part
            if s > 0:
                acc = acc + dh[r, :]
            if s < STAGES_G - 1:
                dh[r, :] = acc
            else:
                acc = acc * scale_out
                dgu[0, r, :] = (acc * act_a[r, :]).astype(BF16)
                dgu[1, r, :] = (acc * act_s[r, :]).astype(BF16)
            return 0

        lax.fori_loop(0, 4, step, 0)

    def in_copy(mat, k):
        q = lax.rem(z + k, 4)
        return pltpu.make_async_remote_copy(
            src_ref=grad_s.at[mat, q], dst_ref=grad_r.at[z, mat],
            send_sem=rs_send.at[mat, k, 0], recv_sem=rs_recv.at[mat, k],
            device_id=(q, e), device_id_type=MESH,
        )

    def in_self(mat):
        return pltpu.make_async_copy(grad_s.at[mat, z], grad_r.at[z, mat], rs_self.at[mat, 0, 0])

    def grad_in(mat):
        def step(j, _):
            k = lax.rem(2 + 3 * j, 4)
            q = lax.rem(z + k, 4)
            rows = xs[:, :, :, :, pl.ds(pl.multiple_of(q * QUARTER, QUARTER), QUARTER)].reshape(ROWS, QUARTER)
            grad_s[mat, q] = (dot(rows, dgu[mat], 0, 0) * scale_in).astype(BF16)

            @pl.when(k != 0)
            def _():
                in_copy(mat, k).start()

            @pl.when(k == 0)
            def _():
                in_self(mat).start()

            return 0

        lax.fori_loop(0, 4, step, 0)

    def rows_back(s):
        def step(m, _):
            r = pl.ds(pl.multiple_of(m * 256, 256), 256)
            for half in range(2):
                col = half * HALF + s * wr
                v = dot(dgu[0, r, :], win[0, col : col + wr, :], 1, 1)
                v = v + dot(dgu[1, r, :], win[1, col : col + wr, :], 1, 1)
                send_x[m, :, :, :, col : col + wr] = (v * scale_in).astype(BF16).reshape(4, 2, CAP, wr)
            return 0

        lax.fori_loop(0, 4, step, 0)

    pairs = [(0, 0), (1, 1), (2, 2), (3, 3), (0, 1), (0, 2), (0, 3), (1, 2), (1, 3), (2, 3)]

    def fold(v):
        total = None
        for i in range(v.shape[0] // 8):
            for j in range(v.shape[1] // 128):
                part = v[i * 8 : (i + 1) * 8, j * 128 : (j + 1) * 128]
                total = part if total is None else total + part
        return total

    def gram_of(mat, sums):
        def step(i, sums):
            r = pl.ds(pl.multiple_of(i * 16, 16), 16)
            g = [grad_r[s, mat, r, :].astype(F32) for s in range(4)]
            return tuple(t + fold(g[a] * g[b]) for t, (a, b) in zip(sums, pairs))

        return lax.fori_loop(0, 32, step, sums)

    load[0].wait()
    gather(tok, send_x, ex[0][4], wx, False)
    pl.semaphore_wait(barrier, 16)
    start_first(ex[0])
    gather(tok, send_x, ex[1][4], wx, False)
    start_first(ex[1])
    load[1].wait()
    gather(cot, send_g, eg[0][4], wg, True)
    gather(cot, send_g, eg[1][4], wg, True)
    forward(ex[0])
    start_first(eg[0])
    gather(cot, send_g, eg[2][4], wg, True)
    gather(cot, send_g, eg[3][4], wg, True)
    forward(ex[1])
    start_first(eg[1])
    forward(eg[0])
    start_first(eg[2])
    load[2].wait()
    load[3].wait()
    arrive(ex[0])
    arrive(ex[1])
    start_first(eg[3])
    each(0, 2, activate)
    forward(eg[1])
    each(2, 4, activate)
    forward(eg[2])
    arrive(eg[0])
    grad_out(0)
    hidden_grad(0)
    arrive(eg[1])
    grad_out(1)
    hidden_grad(1)
    forward(eg[3])
    arrive(eg[2])
    grad_out(2)
    hidden_grad(2)
    arrive(eg[3])
    grad_out(3)
    hidden_grad(3)
    grad_in(0)
    grad_in(1)
    for s in range(STAGES_R):
        rows_back(s)
        start_first(er[s])

    sums = tuple(jnp.zeros((8, 128), F32) for _ in pairs)
    for k in range(1, 4):
        for j in range(QUARTER // wg):
            pltpu.make_async_remote_copy(
                src_ref=grad_s.at[2, 0, :, pl.ds(j * wg, wg)],
                dst_ref=grad_r.at[lax.rem(z - k + 4, 4), 2, :, pl.ds(j * wg, wg)],
                send_sem=rs_send.at[2, 0, 0], recv_sem=rs_recv.at[2 + j, k],
                device_id=(lax.rem(z + k, 4), e), device_id_type=MESH,
            ).wait_recv()
    for s in range(STAGES_G):
        for half in range(2):
            q, remote, local = out_copy(s, half)

            @pl.when(z != q)
            def _():
                remote.wait_send()

            @pl.when(z == q)
            def _():
                local.wait()

    sums = gram_of(2, sums)
    for s in range(STAGES_R):
        forward(er[s])
    for mat in range(2):
        each(1, 4, lambda k: in_copy(mat, k).wait())
        in_self(mat).wait()
        sums = gram_of(mat, sums)

    own = jnp.concatenate([jnp.sum(t, axis=0, keepdims=True) for t in sums] + [jnp.zeros((6, 128), F32)], axis=0)
    gram[z] = own

    def gram_copy(k):
        return pltpu.make_async_remote_copy(
            src_ref=gram.at[z], dst_ref=gram.at[z], send_sem=gram_send.at[k], recv_sem=gram_recv.at[k],
            device_id=(lax.rem(z + k, 4), e), device_id_type=MESH,
        )

    each(1, 4, lambda k: gram_copy(k).start())
    load[4].wait()
    load[5].wait()
    each(1, 4, lambda k: gram_copy(k).wait())
    total = jnp.sum(gram[0] + gram[1] + gram[2] + gram[3], axis=1, keepdims=True)
    dots = {p: total[i : i + 1, :] for i, p in enumerate(pairs)}

    def coefficient(cross, norm):
        return 1.0 - cross / (2.0 * (norm + EPS))

    a0 = coefficient(dots[0, 2], dots[0, 0])
    a2 = coefficient(dots[0, 2], dots[2, 2])
    a1 = coefficient(dots[1, 3], dots[1, 1])
    a3 = coefficient(dots[1, 3], dots[3, 3])
    n0 = a0 * a0 * dots[0, 0] + 2.0 * a0 * a2 * dots[0, 2] + a2 * a2 * dots[2, 2]
    n1 = a1 * a1 * dots[1, 1] + 2.0 * a1 * a3 * dots[1, 3] + a3 * a3 * dots[3, 3]
    cross = a0 * (a1 * dots[0, 1] + a3 * dots[0, 3]) + a2 * (a1 * dots[1, 2] + a3 * dots[2, 3])
    b0 = coefficient(cross, jnp.maximum(n0, 0.0))
    b1 = coefficient(cross, jnp.maximum(n1, 0.0))
    coef = [b0 * a0, b1 * a1, b0 * a2, b1 * a3]

    def slot(mat, hh, owner):
        if mat < 2:
            return nwin_h.at[mat, pl.ds(owner * QUARTER + hh * 256, 256), :]
        return nwout_h.at[pl.ds(hh * 256, 256), pl.ds(pl.multiple_of(owner * QUARTER, QUARTER), QUARTER)]

    def ag_copy(mat, hh, direction):
        return pltpu.make_async_remote_copy(
            src_ref=grad_s.at[mat, 0, pl.ds(hh * 256, 256), :], dst_ref=slot(mat, hh, z),
            send_sem=ag_send.at[direction, 2 * mat + hh], recv_sem=ag_recv.at[direction, 2 * mat + hh],
            device_id=(lax.rem(z + (1 if direction == 0 else 3), 4), e), device_id_type=MESH,
        )

    def fw_copy(mat, hh):
        owner = lax.rem(z + (3 if hh == 0 else 1), 4)
        return pltpu.make_async_remote_copy(
            src_ref=slot(mat, hh, owner), dst_ref=slot(mat, hh, owner),
            send_sem=fw_send.at[2 * mat + hh], recv_sem=fw_recv.at[2 * mat + hh],
            device_id=(lax.rem(z + (1 if hh == 0 else 3), 4), e), device_id_type=MESH,
        )

    def out_local(mat, hh):
        own_w = pltpu.make_async_copy(
            grad_s.at[mat, 0, pl.ds(hh * 256, 256), :], slot(mat, hh, z), out_sem.at[0, 2 * mat + hh]
        )
        if mat < 2:
            own_m = pltpu.make_async_copy(
                mom_in.at[mat, pl.ds(hh * 256, 256), :], nmin_h.at[mat, pl.ds(hh * 256, 256), :],
                out_sem.at[1, 2 * mat + hh],
            )
        else:
            own_m = pltpu.make_async_copy(
                mom_out.at[pl.ds(hh * 256, 256), :], nmout_h.at[pl.ds(hh * 256, 256), :],
                out_sem.at[1, 2 * mat + hh],
            )
        return own_w, own_m

    for mat in range(3):
        for hh in range(2):

            def step(i, _):
                r = pl.multiple_of(hh * 256 + i * 32, 32)
                rr = pl.ds(r, 32)
                comb = coef[0] * grad_r[0, mat, rr, :].astype(F32)
                for s in range(1, 4):
                    comb = comb + coef[s] * grad_r[s, mat, rr, :].astype(F32)
                if mat < 2:
                    new = MOMENTUM * mom_in[mat, rr, :] + comb
                    mom_in[mat, rr, :] = new
                    old = win[mat, pl.ds(pl.multiple_of(z * QUARTER + r, 32), 32), :]
                else:
                    new = MOMENTUM * mom_out[rr, :] + comb
                    mom_out[rr, :] = new
                    old = wout[rr, pl.ds(pl.multiple_of(z * QUARTER, QUARTER), QUARTER)]
                grad_s[mat, 0, rr, :] = (old.astype(F32) - RATE * new).astype(BF16)
                return 0

            lax.fori_loop(0, 8, step, 0)
            ag_copy(mat, hh, 0).start()
            ag_copy(mat, hh, 1).start()
            for copy in out_local(mat, hh):
                copy.start()

    def pass_on(mat, hh):
        ag_copy(mat, hh, hh).wait_recv()
        fw_copy(mat, hh).start()

    pass_on(0, 0)
    pass_on(0, 1)

    for s in range(STAGES_R):
        arrive(er[s])

    def tokens_step(n, _):
        cols = pl.ds(pl.multiple_of(n * 512, 512), 512)
        rows = send_g[:, :, :, :, cols].reshape(ROWS, 512)
        tok[:, cols] = dot(onehot[...], rows, 0, 0).astype(BF16)
        return 0

    lax.fori_loop(0, 4, tokens_step, 0)
    tok_out = pltpu.make_async_copy(tok, tg_h, load_sem.at[0])
    tok_out.start()

    for mat in range(1, 3):
        for hh in range(2):
            pass_on(mat, hh)
    for mat in range(3):
        for hh in range(2):
            ag_copy(mat, hh, 1 - hh).wait_recv()
            ag_copy(mat, hh, 0).wait_send()
            ag_copy(mat, hh, 1).wait_send()
            fw_copy(mat, hh).wait()
            for copy in out_local(mat, hh):
                copy.wait()
    tok_out.wait()


def shards(tokens, cotangent, slot_rows, slot_count, slot_weight, w_in, w_out, momentum_in, momentum_out):
    any_ = pl.BlockSpec(memory_space=pl.ANY)
    vmem = pl.BlockSpec(memory_space=pltpu.VMEM)
    stages = STAGES_X + STAGES_G + STAGES_R
    grid5 = (4, 4, 2, CAP, D)
    mid = (2, 4, 4, 2, CAP, HALF)
    dma = pltpu.SemaphoreType.DMA
    outs = pl.pallas_call(
        kernel,
        out_shape=(
            jax.ShapeDtypeStruct((256, D), BF16),
            jax.ShapeDtypeStruct((2, D, FF), BF16),
            jax.ShapeDtypeStruct((FF, D), BF16),
            jax.ShapeDtypeStruct((2, QUARTER, FF), F32),
            jax.ShapeDtypeStruct((FF, QUARTER), F32),
        ),
        in_specs=[any_, any_, vmem, vmem, vmem, any_, any_, any_, any_],
        out_specs=(any_, any_, any_, any_, any_),
        scratch_shapes=[
            pltpu.VMEM((256, D), BF16),
            pltpu.VMEM((256, D), BF16),
            pltpu.VMEM((ROWS, 256), BF16),
            pltpu.VMEM((ROWS, 128), F32),
            pltpu.VMEM(grid5, BF16),
            pltpu.VMEM(grid5, BF16),
            pltpu.VMEM(mid, BF16),
            pltpu.VMEM(mid, BF16),
            pltpu.VMEM(grid5, BF16),
            pltpu.VMEM(grid5, BF16),
            pltpu.VMEM((2, D, FF), BF16),
            pltpu.VMEM((FF, D), BF16),
            pltpu.VMEM((ROWS, FF), F32),
            pltpu.VMEM((ROWS, FF), F32),
            pltpu.VMEM((ROWS, FF), BF16),
            pltpu.VMEM((ROWS, FF), F32),
            pltpu.VMEM((2, ROWS, FF), BF16),
            pltpu.VMEM((3, 4, QUARTER, QUARTER), BF16),
            pltpu.VMEM((4, 3, QUARTER, QUARTER), BF16),
            pltpu.VMEM((2, QUARTER, FF), F32),
            pltpu.VMEM((FF, QUARTER), F32),
            pltpu.VMEM((4, 16, 128), F32),
            dma((6,)),
            dma((stages, 2, 8)),
            dma((stages, 2, 8)),
            dma((stages, 2, 4)),
            dma((stages, 2, 4)),
            dma((stages, 2)),
            dma((stages, 2)),
            dma((3, STAGES_G, 2)),
            dma((4, 4)),
            dma((3, STAGES_G, 2)),
            dma((4,)),
            dma((4,)),
            dma((2, 6)),
            dma((2, 6)),
            dma((6,)),
            dma((6,)),
            dma((2, 6)),
        ],
        compiler_params=pltpu.CompilerParams(
            collective_id=0, has_side_effects=True, vmem_limit_bytes=62 << 20
        ),
        name="step",
    )(
        tokens[0], cotangent[0], slot_rows[0, 0].T, slot_count[0], slot_weight[0, 0].T,
        w_in[0], w_out[0], momentum_in[0], momentum_out[0],
    )
    return tuple(o[None] for o in outs)


def solution(mesh):
    return jax.shard_map(
        shards,
        mesh=mesh,
        in_specs=(
            P("dp", "expert", None),
            P("dp", "expert", None),
            P("dp", "expert", None, None),
            P("dp", "expert", None),
            P("dp", "expert", None, None),
            P("expert", None, None, None),
            P("expert", None, None),
            P("expert", None, "dp", None),
            P("expert", None, "dp"),
        ),
        out_specs=(
            P("dp", "expert", None),
            P("expert", None, None, None),
            P("expert", None, None),
            P("expert", None, "dp", None),
            P("expert", None, "dp"),
        ),
        check_vma=False,
    )
```

profile of v0, /device:TPU:0, one launch (start us, length us, event | category | flops | bytes accessed | tf_op | source)
XLA Modules:
  0.0 241.2 jit_solution(14151732597380137643)
XLA Ops:
  0.6 1.4 copy.14
  2.0 1.4 copy.15
  3.4 225.6 %step.1 = (bf16[256,2048]{1,0:T(8,128)(2,1)}, bf16[2,2048,512]{2,1,0:T(8,128)(2,1)}, bf16[512,2048]{1,0:T(8,128)(2,1)}, f32[2,512,512]{2,1,0:T(8,128)}, f32[512,512]{1,0:T(8,128)}) custom-call(bf16[256,2048]{1,0:T(8,128)(2,1)} %bitcast.24, bf16[256,2048]{1,0:T(8,128)(2,1)} %bitcast.25, s32[32,32]{1,0:T(8,128)} %bitcast.29, s32[1,32]{1,0:T(1,128)} %bitcast.31, ...), custom_call_target="tpu_custom_call" | custom-call | tf_op jit(solution)/shard_map/step/pallas_call | solution.py:515
  229.0 2.3 copy.21
  231.3 0.0 copy-start.1
  231.3 4.6 %copy.22 = bf16[1,2,2048,512]{3,2,1,0:T(8,128)(2,1)} copy(bf16[1,2,2048,512]{3,2,1,0:T(8,128)(2,1)} %bitcast.19) | data formatting | bytes 8388608
  235.9 0.0 copy-done.1
  235.9 0.0 copy-start
  235.9 1.3 copy.23
  237.3 1.0 copy-done
  238.3 0.0 copy-start.2
  238.3 1.3 copy.24
  239.6 0.6 copy-done.2
  240.3 1.0 copy.25
Async XLA Ops:
  231.3 4.6 %copy-start.1 = (bf16[512,2048]{1,0:T(8,128)(2,1)S(1)}, bf16[512,2048]{1,0:T(8,128)(2,1)}, u32[]{:S(2)}) copy-start(bf16[512,2048]{1,0:T(8,128)(2,1)} %get-tuple-element.12) | copy-start | bytes 6291460
  235.9 2.3 copy-start
  238.3 2.0 copy-start.2
where the time goes:
time: 242 us; the launch traced here: 241 us
  Pallas kernels  226 us (93%)
  local copies, waits for them, and re-layouts  15 us (6%)
    pallas_call x1, Pallas kernels, shards(): pl.pallas_call(kernel, out_shape=(jax.ShapeDtypeStruct((256, D), BF16), j...  226 us
    unnamed x13, local copies, waits for them, and re-layouts  15 us

commit v1 on v0

--- a/solution.py
+++ b/solution.py
@@ -19,6 +19,7 @@
 STAGES_G = 4
 STAGES_R = 2
 ROWS = 1024
+ORDER_G = (0, 512, 256, 768)
 BF16 = jnp.bfloat16
 F32 = jnp.float32
 
@@ -29,11 +30,11 @@
 
 def kernel(
     tok_h, cot_h, rows_v, count_v, weight_v, win_h, wout_h, min_h, mout_h,
-    tg_h, nwin_h, nwout_h, nmin_h, nmout_h,
-    tok, cot, onehot, scale, send_x, send_g, mid_x, mid_g, xs, gs_, win, wout,
-    act_a, act_s, hid, dh, dgu, grad_s, grad_r, mom_in, mom_out, gram,
+    tok, xs, nwout, mom_in, mom_out,
+    cot, onehot, scale, send_x, send_g, mid_x, mid_g, gs_, win, wout,
+    act_a, act_s, hid, dh, dgu, grad_s, grad_r, gram,
     load_sem, p1_send, p1_recv, p2_send, p2_recv, self1, self2,
-    rs_send, rs_recv, rs_self, gram_send, gram_recv, ag_send, ag_recv, fw_send, fw_recv, out_sem,
+    rs_send, rs_recv, rs_self, gram_send, gram_recv, ag_send, ag_recv, fw_send, fw_recv,
 ):
     z = lax.axis_index("dp")
     e = lax.axis_index("expert")
@@ -50,7 +51,7 @@
         (tok_h, tok), (cot_h, cot), (win_h, win), (wout_h, wout), (min_h, mom_in), (mout_h, mom_out),
     ]
     load = [pltpu.make_async_copy(s, d, load_sem.at[i]) for i, (s, d) in enumerate(loads)]
-    for copy in load:
+    for copy in load[:2]:
         copy.start()
 
     barrier = pltpu.get_barrier_semaphore()
@@ -65,8 +66,8 @@
     for k in range(1, 4):
         greet((lax.rem(z + k, 4), e))
 
-    rows_t = rows_v[...]
-    weight_t = weight_v[...]
+    rows_t = jnp.transpose(rows_v[...])
+    weight_t = jnp.transpose(weight_v[...])
     valid = lax.broadcasted_iota(jnp.int32, (CAP, 32), 0) < count_v[...]
     scale_t = jnp.where(valid, weight_t, 0.0)
     lane = lax.broadcasted_iota(jnp.int32, (CAP, 256), 1)
@@ -125,12 +126,12 @@
             pa = lax.rem(y + k, 4)
             peer = expert_id(x, pa, c)
             src = mid.at[0, pa, :, :, :, mcol]
-            dst = fin.at[:, y, :, :, col]
+            dst = fin.at[:, y, :, :, col] if fin is not xs else fin.at[c0 // QUARTER, :, y]
         else:
             pa = lax.rem(x + k, 4)
             peer = expert_id(pa, y, c)
             src = mid.at[1, pa, :, :, :, mcol]
-            dst = fin.at[x, :, :, :, col]
+            dst = fin.at[x, :, :, :, col] if fin is not xs else fin.at[2 + c0 // QUARTER, x]
         return pltpu.make_async_remote_copy(
             src_ref=src, dst_ref=dst, send_sem=p2_send.at[st, half, k], recv_sem=p2_recv.at[st, half, k],
             device_id=(z, peer), device_id_type=MESH,
@@ -140,12 +141,10 @@
         col = pl.ds(half * HALF + c0, w)
         mcol = pl.ds(c0, w)
         if half == 0:
-            return pltpu.make_async_copy(
-                mid.at[0, y, :, :, :, mcol], fin.at[:, y, :, :, col], self2.at[st, half]
-            )
-        return pltpu.make_async_copy(
-            mid.at[1, x, :, :, :, mcol], fin.at[x, :, :, :, col], self2.at[st, half]
-        )
+            dst = fin.at[:, y, :, :, col] if fin is not xs else fin.at[c0 // QUARTER, :, y]
+            return pltpu.make_async_copy(mid.at[0, y, :, :, :, mcol], dst, self2.at[st, half])
+        dst = fin.at[x, :, :, :, col] if fin is not xs else fin.at[2 + c0 // QUARTER, x]
+        return pltpu.make_async_copy(mid.at[1, x, :, :, :, mcol], dst, self2.at[st, half])
 
     def each(lo, hi, fn):
         def step(k, _):
@@ -181,11 +180,11 @@
 
     wx, wg, wr = HALF // STAGES_X, HALF // STAGES_G, HALF // STAGES_R
     ex = [(send_x, mid_x, xs, s, s * wx, wx) for s in range(STAGES_X)]
-    eg = [(send_g, mid_g, gs_, STAGES_X + s, s * wg, wg) for s in range(STAGES_G)]
+    eg = [(send_g, mid_g, gs_, STAGES_X + s, ORDER_G[s], wg) for s in range(STAGES_G)]
     er = [(send_x, mid_x, send_g, STAGES_X + STAGES_G + s, s * wr, wr) for s in range(STAGES_R)]
 
     def activate(m):
-        rows = xs[m].reshape(256, D)
+        rows = jnp.concatenate([xs[b, m].reshape(256, QUARTER) for b in range(4)], axis=1)
         r = pl.ds(pl.multiple_of(m * 256, 256), 256)
         gate = dot(rows, win[0], 1, 0) * scale_in
         up = dot(rows, win[1], 1, 0) * scale_in
@@ -196,7 +195,7 @@
         act_s[r, :] = act
 
     def out_copy(s, half):
-        col = half * HALF + s * wg
+        col = half * HALF + ORDER_G[s]
         q, off = col // QUARTER, col % QUARTER
         return q, pltpu.make_async_remote_copy(
             src_ref=grad_s.at[2, q, :, pl.ds(off, wg)],
@@ -210,7 +209,7 @@
 
     def grad_out(s):
         for half in range(2):
-            col = half * HALF + s * wg
+            col = half * HALF + ORDER_G[s]
             q, off = col // QUARTER, col % QUARTER
             rows = gs_[:, :, :, :, col : col + wg].reshape(ROWS, wg)
             grad_s[2, q, :, off : off + wg] = (dot(hid[...], rows, 0, 0) * scale_out).astype(BF16)
@@ -229,7 +228,7 @@
             r = pl.ds(pl.multiple_of(m * 256, 256), 256)
             acc = None
             for half in range(2):
-                col = half * HALF + s * wg
+                col = half * HALF + ORDER_G[s]
                 rows = gs_[m, :, :, :, col : col + wg].reshape(256, wg)
                 part = dot(rows, wout[:, col : col + wg], 1, 1)
                 acc = part if acc is None else acc + part
@@ -260,7 +259,7 @@
         def step(j, _):
             k = lax.rem(2 + 3 * j, 4)
             q = lax.rem(z + k, 4)
-            rows = xs[:, :, :, :, pl.ds(pl.multiple_of(q * QUARTER, QUARTER), QUARTER)].reshape(ROWS, QUARTER)
+            rows = xs[q].reshape(ROWS, QUARTER)
             grad_s[mat, q] = (dot(rows, dgu[mat], 0, 0) * scale_in).astype(BF16)
 
             @pl.when(k != 0)
@@ -309,6 +308,8 @@
     gather(tok, send_x, ex[0][4], wx, False)
     pl.semaphore_wait(barrier, 16)
     start_first(ex[0])
+    for copy in load[2:]:
+        copy.start()
     gather(tok, send_x, ex[1][4], wx, False)
     start_first(ex[1])
     load[1].wait()
@@ -411,12 +412,12 @@
 
     def slot(mat, hh, owner):
         if mat < 2:
-            return nwin_h.at[mat, pl.ds(owner * QUARTER + hh * 256, 256), :]
-        return nwout_h.at[pl.ds(hh * 256, 256), pl.ds(pl.multiple_of(owner * QUARTER, QUARTER), QUARTER)]
+            return xs.at[2 * mat + owner // 2, 2 * lax.rem(owner, 2) + hh]
+        return nwout.at[pl.ds(hh * 256, 256), pl.ds(pl.multiple_of(owner * QUARTER, QUARTER), QUARTER)]
 
     def ag_copy(mat, hh, direction):
         return pltpu.make_async_remote_copy(
-            src_ref=grad_s.at[mat, 0, pl.ds(hh * 256, 256), :], dst_ref=slot(mat, hh, z),
+            src_ref=slot(mat, hh, z), dst_ref=slot(mat, hh, z),
             send_sem=ag_send.at[direction, 2 * mat + hh], recv_sem=ag_recv.at[direction, 2 * mat + hh],
             device_id=(lax.rem(z + (1 if direction == 0 else 3), 4), e), device_id_type=MESH,
         )
@@ -428,22 +429,6 @@
             send_sem=fw_send.at[2 * mat + hh], recv_sem=fw_recv.at[2 * mat + hh],
             device_id=(lax.rem(z + (1 if hh == 0 else 3), 4), e), device_id_type=MESH,
         )
-
-    def out_local(mat, hh):
-        own_w = pltpu.make_async_copy(
-            grad_s.at[mat, 0, pl.ds(hh * 256, 256), :], slot(mat, hh, z), out_sem.at[0, 2 * mat + hh]
-        )
-        if mat < 2:
-            own_m = pltpu.make_async_copy(
-                mom_in.at[mat, pl.ds(hh * 256, 256), :], nmin_h.at[mat, pl.ds(hh * 256, 256), :],
-                out_sem.at[1, 2 * mat + hh],
-            )
-        else:
-            own_m = pltpu.make_async_copy(
-                mom_out.at[pl.ds(hh * 256, 256), :], nmout_h.at[pl.ds(hh * 256, 256), :],
-                out_sem.at[1, 2 * mat + hh],
-            )
-        return own_w, own_m
 
     for mat in range(3):
         for hh in range(2):
@@ -462,14 +447,16 @@
                     new = MOMENTUM * mom_out[rr, :] + comb
                     mom_out[rr, :] = new
                     old = wout[rr, pl.ds(pl.multiple_of(z * QUARTER, QUARTER), QUARTER)]
-                grad_s[mat, 0, rr, :] = (old.astype(F32) - RATE * new).astype(BF16)
+                value = (old.astype(F32) - RATE * new).astype(BF16)
+                if mat < 2:
+                    xs[2 * mat + z // 2, 2 * lax.rem(z, 2) + hh, i // 2, lax.rem(i, 2)] = value
+                else:
+                    nwout[rr, pl.ds(pl.multiple_of(z * QUARTER, QUARTER), QUARTER)] = value
                 return 0
 
             lax.fori_loop(0, 8, step, 0)
             ag_copy(mat, hh, 0).start()
             ag_copy(mat, hh, 1).start()
-            for copy in out_local(mat, hh):
-                copy.start()
 
     def pass_on(mat, hh):
         ag_copy(mat, hh, hh).wait_recv()
@@ -488,8 +475,6 @@
         return 0
 
     lax.fori_loop(0, 4, tokens_step, 0)
-    tok_out = pltpu.make_async_copy(tok, tg_h, load_sem.at[0])
-    tok_out.start()
 
     for mat in range(1, 3):
         for hh in range(2):
@@ -500,9 +485,6 @@
             ag_copy(mat, hh, 0).wait_send()
             ag_copy(mat, hh, 1).wait_send()
             fw_copy(mat, hh).wait()
-            for copy in out_local(mat, hh):
-                copy.wait()
-    tok_out.wait()
 
 
 def shards(tokens, cotangent, slot_rows, slot_count, slot_weight, w_in, w_out, momentum_in, momentum_out):
@@ -515,16 +497,15 @@
     outs = pl.pallas_call(
         kernel,
         out_shape=(
-            jax.ShapeDtypeStruct((256, D), BF16),
-            jax.ShapeDtypeStruct((2, D, FF), BF16),
-            jax.ShapeDtypeStruct((FF, D), BF16),
-            jax.ShapeDtypeStruct((2, QUARTER, FF), F32),
-            jax.ShapeDtypeStruct((FF, QUARTER), F32),
+            pltpu.VMEM((256, D), BF16),
+            pltpu.VMEM((4, 4, 4, 2, CAP, QUARTER), BF16),
+            pltpu.VMEM((FF, D), BF16),
+            pltpu.VMEM((2, QUARTER, FF), F32),
+            pltpu.VMEM((FF, QUARTER), F32),
         ),
         in_specs=[any_, any_, vmem, vmem, vmem, any_, any_, any_, any_],
-        out_specs=(any_, any_, any_, any_, any_),
+        out_specs=(vmem,) * 5,
         scratch_shapes=[
-            pltpu.VMEM((256, D), BF16),
             pltpu.VMEM((256, D), BF16),
             pltpu.VMEM((ROWS, 256), BF16),
             pltpu.VMEM((ROWS, 128), F32),
@@ -532,7 +513,6 @@
             pltpu.VMEM(grid5, BF16),
             pltpu.VMEM(mid, BF16),
             pltpu.VMEM(mid, BF16),
-            pltpu.VMEM(grid5, BF16),
             pltpu.VMEM(grid5, BF16),
             pltpu.VMEM((2, D, FF), BF16),
             pltpu.VMEM((FF, D), BF16),
@@ -543,8 +523,6 @@
             pltpu.VMEM((2, ROWS, FF), BF16),
             pltpu.VMEM((3, 4, QUARTER, QUARTER), BF16),
             pltpu.VMEM((4, 3, QUARTER, QUARTER), BF16),
-            pltpu.VMEM((2, QUARTER, FF), F32),
-            pltpu.VMEM((FF, QUARTER), F32),
             pltpu.VMEM((4, 16, 128), F32),
             dma((6,)),
             dma((stages, 2, 8)),
@@ -562,16 +540,16 @@
             dma((2, 6)),
             dma((6,)),
             dma((6,)),
-            dma((2, 6)),
         ],
         compiler_params=pltpu.CompilerParams(
-            collective_id=0, has_side_effects=True, vmem_limit_bytes=62 << 20
+            collective_id=0, has_side_effects=True, vmem_limit_bytes=53 << 20
         ),
         name="step",
     )(
-        tokens[0], cotangent[0], slot_rows[0, 0].T, slot_count[0], slot_weight[0, 0].T,
+        tokens[0], cotangent[0], slot_rows[0, 0], slot_count[0], slot_weight[0, 0],
         w_in[0], w_out[0], momentum_in[0], momentum_out[0],
     )
+    outs = (outs[0], outs[1].reshape(2, D, FF)) + tuple(outs[2:])
     return tuple(o[None] for o in outs)
 
 

time: 242 us -> 227 us (0.938)
  local copies, waits for them, and re-layouts: 15 us -> 6.59 us
  Pallas kernels: 226 us -> 220 us
    unnamed x13 -> x5, local copies, waits for them, and re-layouts: 15 us -> 6.59 us
    pallas_call x1, Pallas kernels: 226 us -> 220 us  [shards(): pl.pallas_call(kernel, out_shape=(pltpu.VMEM((256, D), BF16), pltpu.VMEM(...]
where the time goes in v1:
time: 227 us
  Pallas kernels  220 us (97%)
  local copies, waits for them, and re-layouts  6.59 us (3%)
    pallas_call x1, Pallas kernels, shards(): pl.pallas_call(kernel, out_shape=(pltpu.VMEM((256, D), BF16), pltpu.VMEM(...  220 us
    unnamed x5, local copies, waits for them, and re-layouts  6.59 us

profile of v1, /device:TPU:0, one launch (start us, length us, event | category | flops | bytes accessed | tf_op | source)
XLA Modules:
  0.0 227.2 jit_solution(1751805543220401913)
XLA Ops:
  0.6 219.9 %step.1 = (bf16[256,2048]{1,0:T(8,128)(2,1)S(1)}, bf16[4,4,4,2,32,512]{5,4,3,2,1,0:T(8,128)(2,1)S(1)}, bf16[512,2048]{1,0:T(8,128)(2,1)S(1)}, f32[2,512,512]{2,1,0:T(8,128)S(1)}, f32[512,512]{1,0:T(8,128)S(1)}) custom-call(bf16[256,2048]{1,0:T(8,128)(2,1)} %bitcast.22, bf16[256,2048]{1,0:T(8,128)(2,1)} %bitcast.23, s32[32,32]{1,0:T(8,128)} %bitcast.25, ...), custom_call_target="tpu_custom_call" | custom-call | tf_op jit(solution)/shard_map/step/pallas_call | solution.py:497
  220.6 1.0 copy.19
  221.5 2.0 copy.20
  223.5 1.0 copy.23
  224.5 1.3 copy.21
  225.8 1.3 copy.22

commit v2 on v1

--- a/solution.py
+++ b/solution.py
@@ -19,7 +19,6 @@
 STAGES_G = 4
 STAGES_R = 2
 ROWS = 1024
-ORDER_G = (0, 512, 256, 768)
 BF16 = jnp.bfloat16
 F32 = jnp.float32
 
@@ -79,72 +78,69 @@
         def step(m, _):
             r0 = pl.multiple_of(m * 256, 256)
             hot = onehot[pl.ds(r0, 256), :]
-            for half in range(2):
-                col = half * HALF + c0
-                v = dot(hot, src[:, col : col + w], 1, 0)
-                if scaled:
+            if scaled:
+                for q in range(4):
+                    v = dot(hot, src[:, q * QUARTER + c0 : q * QUARTER + c0 + w], 1, 0)
                     v = v * scale[pl.ds(r0, 256), 0:1]
-                dst[m, :, :, :, col : col + w] = v.astype(BF16).reshape(4, 2, CAP, w)
+                    dst[q, m, :, :, :, c0 : c0 + w] = v.astype(BF16).reshape(4, 2, CAP, w)
+            else:
+                for half in range(2):
+                    col = half * HALF + c0
+                    v = dot(hot, src[:, col : col + w], 1, 0)
+                    dst[m, :, :, :, col : col + w] = v.astype(BF16).reshape(4, 2, CAP, w)
             return 0
 
         lax.fori_loop(0, 4, step, 0)
+
+    def first_views(send, mid, c0, w, half, pa, pc):
+        if send is send_g:
+            col, both = pl.ds(c0, w), pl.ds(2 * half, 2)
+            if half == 0:
+                return send.at[both, pa, :, pc, :, col], mid.at[0, :, :, x, c, :, col]
+            return send.at[both, :, pa, pc, :, col], mid.at[1, :, :, y, c, :, col]
+        col, mcol = pl.ds(half * HALF + c0, w), pl.ds(c0, w)
+        if half == 0:
+            return send.at[pa, :, pc, :, col], mid.at[0, :, x, c, :, mcol]
+        return send.at[:, pa, pc, :, col], mid.at[1, :, y, c, :, mcol]
+
+    def second_views(mid, fin, c0, w, half, pa):
+        if mid is mid_g:
+            col, both = pl.ds(c0, w), pl.ds(2 * half, 2)
+            src = mid.at[half, :, pa, :, :, :, col]
+            if half == 0:
+                return src, fin.at[both, :, y, :, :, col]
+            return src, fin.at[both, x, :, :, :, col]
+        src = mid.at[half, pa, :, :, :, pl.ds(c0, w)]
+        if half == 0:
+            return src, fin.at[c0 // QUARTER, :, y]
+        return src, fin.at[2 + c0 // QUARTER, x]
 
     def p1_copy(send, mid, st, c0, w, half, k):
         pc = lax.rem(c + lax.rem(k, 2), 2)
-        col = pl.ds(half * HALF + c0, w)
-        mcol = pl.ds(c0, w)
-        if half == 0:
-            pa = lax.rem(x + k // 2, 4)
-            peer = expert_id(pa, y, pc)
-            src = send.at[pa, :, pc, :, col]
-            dst = mid.at[0, :, x, c, :, mcol]
-        else:
-            pa = lax.rem(y + k // 2, 4)
-            peer = expert_id(x, pa, pc)
-            src = send.at[:, pa, pc, :, col]
-            dst = mid.at[1, :, y, c, :, mcol]
+        pa = lax.rem((x if half == 0 else y) + k // 2, 4)
+        peer = expert_id(pa, y, pc) if half == 0 else expert_id(x, pa, pc)
+        src, dst = first_views(send, mid, c0, w, half, pa, pc)
         return pltpu.make_async_remote_copy(
             src_ref=src, dst_ref=dst, send_sem=p1_send.at[st, half, k], recv_sem=p1_recv.at[st, half, k],
             device_id=(z, peer), device_id_type=MESH,
         )
 
     def p1_self(send, mid, st, c0, w, half):
-        col = pl.ds(half * HALF + c0, w)
-        mcol = pl.ds(c0, w)
-        if half == 0:
-            return pltpu.make_async_copy(
-                send.at[x, :, c, :, col], mid.at[0, :, x, c, :, mcol], self1.at[st, half]
-            )
-        return pltpu.make_async_copy(
-            send.at[:, y, c, :, col], mid.at[1, :, y, c, :, mcol], self1.at[st, half]
-        )
+        src, dst = first_views(send, mid, c0, w, half, x if half == 0 else y, c)
+        return pltpu.make_async_copy(src, dst, self1.at[st, half])
 
     def p2_copy(mid, fin, st, c0, w, half, k):
-        col = pl.ds(half * HALF + c0, w)
-        mcol = pl.ds(c0, w)
-        if half == 0:
-            pa = lax.rem(y + k, 4)
-            peer = expert_id(x, pa, c)
-            src = mid.at[0, pa, :, :, :, mcol]
-            dst = fin.at[:, y, :, :, col] if fin is not xs else fin.at[c0 // QUARTER, :, y]
-        else:
-            pa = lax.rem(x + k, 4)
-            peer = expert_id(pa, y, c)
-            src = mid.at[1, pa, :, :, :, mcol]
-            dst = fin.at[x, :, :, :, col] if fin is not xs else fin.at[2 + c0 // QUARTER, x]
+        pa = lax.rem((y if half == 0 else x) + k, 4)
+        peer = expert_id(x, pa, c) if half == 0 else expert_id(pa, y, c)
+        src, dst = second_views(mid, fin, c0, w, half, pa)
         return pltpu.make_async_remote_copy(
             src_ref=src, dst_ref=dst, send_sem=p2_send.at[st, half, k], recv_sem=p2_recv.at[st, half, k],
             device_id=(z, peer), device_id_type=MESH,
         )
 
     def p2_self(mid, fin, st, c0, w, half):
-        col = pl.ds(half * HALF + c0, w)
-        mcol = pl.ds(c0, w)
-        if half == 0:
-            dst = fin.at[:, y, :, :, col] if fin is not xs else fin.at[c0 // QUARTER, :, y]
-            return pltpu.make_async_copy(mid.at[0, y, :, :, :, mcol], dst, self2.at[st, half])
-        dst = fin.at[x, :, :, :, col] if fin is not xs else fin.at[2 + c0 // QUARTER, x]
-        return pltpu.make_async_copy(mid.at[1, x, :, :, :, mcol], dst, self2.at[st, half])
+        src, dst = second_views(mid, fin, c0, w, half, y if half == 0 else x)
+        return pltpu.make_async_copy(src, dst, self2.at[st, half])
 
     def each(lo, hi, fn):
         def step(k, _):
@@ -178,9 +174,9 @@
             each(1, 4, lambda k: p2_copy(mid, fin, st, c0, w, half, k).wait())
             p2_self(mid, fin, st, c0, w, half).wait()
 
-    wx, wg, wr = HALF // STAGES_X, HALF // STAGES_G, HALF // STAGES_R
+    wx, wg, wr = HALF // STAGES_X, QUARTER // STAGES_G, HALF // STAGES_R
     ex = [(send_x, mid_x, xs, s, s * wx, wx) for s in range(STAGES_X)]
-    eg = [(send_g, mid_g, gs_, STAGES_X + s, ORDER_G[s], wg) for s in range(STAGES_G)]
+    eg = [(send_g, mid_g, gs_, STAGES_X + s, s * wg, wg) for s in range(STAGES_G)]
     er = [(send_x, mid_x, send_g, STAGES_X + STAGES_G + s, s * wr, wr) for s in range(STAGES_R)]
 
     def activate(m):
@@ -194,26 +190,21 @@
         act_a[r, :] = up * sig * (1.0 + gate * (1.0 - sig))
         act_s[r, :] = act
 
-    def out_copy(s, half):
-        col = half * HALF + ORDER_G[s]
-        q, off = col // QUARTER, col % QUARTER
-        return q, pltpu.make_async_remote_copy(
-            src_ref=grad_s.at[2, q, :, pl.ds(off, wg)],
-            dst_ref=grad_r.at[z, 2, :, pl.ds(off, wg)],
-            send_sem=rs_send.at[2, s, half],
-            recv_sem=rs_recv.at[2 + off // wg, lax.rem(q - z + 4, 4)],
-            device_id=(q, e), device_id_type=MESH,
-        ), pltpu.make_async_copy(
-            grad_s.at[2, q, :, pl.ds(off, wg)], grad_r.at[z, 2, :, pl.ds(off, wg)], rs_self.at[2, s, half]
-        )
+    def out_copy(s, q):
+        src = grad_s.at[2, q, :, pl.ds(s * wg, wg)]
+        dst = grad_r.at[z, 2, :, pl.ds(s * wg, wg)]
+        return pltpu.make_async_remote_copy(
+            src_ref=src, dst_ref=dst, send_sem=rs_send.at[2 + s, q],
+            recv_sem=rs_recv.at[2 + s, lax.rem(q - z + 4, 4)], device_id=(q, e), device_id_type=MESH,
+        ), pltpu.make_async_copy(src, dst, rs_self.at[2 + s])
 
     def grad_out(s):
-        for half in range(2):
-            col = half * HALF + ORDER_G[s]
-            q, off = col // QUARTER, col % QUARTER
-            rows = gs_[:, :, :, :, col : col + wg].reshape(ROWS, wg)
-            grad_s[2, q, :, off : off + wg] = (dot(hid[...], rows, 0, 0) * scale_out).astype(BF16)
-            q, remote, local = out_copy(s, half)
+        cols = slice(s * wg, s * wg + wg)
+        rows = jnp.concatenate([gs_[q, :, :, :, :, cols].reshape(ROWS, wg) for q in range(4)], axis=1)
+        out = (dot(hid[...], rows, 0, 0) * scale_out).astype(BF16)
+        for q in range(4):
+            grad_s[2, q, :, cols] = out[:, q * wg : (q + 1) * wg]
+            remote, local = out_copy(s, q)
 
             @pl.when(z != q)
             def _():
@@ -226,12 +217,12 @@
     def hidden_grad(s):
         def step(m, _):
             r = pl.ds(pl.multiple_of(m * 256, 256), 256)
-            acc = None
-            for half in range(2):
-                col = half * HALF + ORDER_G[s]
-                rows = gs_[m, :, :, :, col : col + wg].reshape(256, wg)
-                part = dot(rows, wout[:, col : col + wg], 1, 1)
-                acc = part if acc is None else acc + part
+            cols = slice(s * wg, s * wg + wg)
+            rows = jnp.concatenate([gs_[q, m, :, :, :, cols].reshape(256, wg) for q in range(4)], axis=1)
+            down = jnp.concatenate(
+                [wout[:, q * QUARTER + s * wg : q * QUARTER + s * wg + wg] for q in range(4)], axis=1
+            )
+            acc = dot(rows, down, 1, 1)
             if s > 0:
                 acc = acc + dh[r, :]
             if s < STAGES_G - 1:
@@ -248,12 +239,12 @@
         q = lax.rem(z + k, 4)
         return pltpu.make_async_remote_copy(
             src_ref=grad_s.at[mat, q], dst_ref=grad_r.at[z, mat],
-            send_sem=rs_send.at[mat, k, 0], recv_sem=rs_recv.at[mat, k],
+            send_sem=rs_send.at[mat, k], recv_sem=rs_recv.at[mat, k],
             device_id=(q, e), device_id_type=MESH,
         )
 
     def in_self(mat):
-        return pltpu.make_async_copy(grad_s.at[mat, z], grad_r.at[z, mat], rs_self.at[mat, 0, 0])
+        return pltpu.make_async_copy(grad_s.at[mat, z], grad_r.at[z, mat], rs_self.at[mat])
 
     def grad_in(mat):
         def step(j, _):
@@ -353,16 +344,16 @@
 
     sums = tuple(jnp.zeros((8, 128), F32) for _ in pairs)
     for k in range(1, 4):
-        for j in range(QUARTER // wg):
+        for j in range(STAGES_G):
             pltpu.make_async_remote_copy(
                 src_ref=grad_s.at[2, 0, :, pl.ds(j * wg, wg)],
                 dst_ref=grad_r.at[lax.rem(z - k + 4, 4), 2, :, pl.ds(j * wg, wg)],
-                send_sem=rs_send.at[2, 0, 0], recv_sem=rs_recv.at[2 + j, k],
+                send_sem=rs_send.at[2 + j, k], recv_sem=rs_recv.at[2 + j, k],
                 device_id=(lax.rem(z + k, 4), e), device_id_type=MESH,
             ).wait_recv()
     for s in range(STAGES_G):
-        for half in range(2):
-            q, remote, local = out_copy(s, half)
+        for q in range(4):
+            remote, local = out_copy(s, q)
 
             @pl.when(z != q)
             def _():
@@ -470,7 +461,7 @@
 
     def tokens_step(n, _):
         cols = pl.ds(pl.multiple_of(n * 512, 512), 512)
-        rows = send_g[:, :, :, :, cols].reshape(ROWS, 512)
+        rows = send_g[n].reshape(ROWS, 512)
         tok[:, cols] = dot(onehot[...], rows, 0, 0).astype(BF16)
         return 0
 
@@ -487,18 +478,35 @@
             fw_copy(mat, hh).wait()
 
 
+def write_out(*refs):
+    sources, targets, sem = refs[:5], refs[5:10], refs[10]
+    copies = []
+    for source, target in zip(sources, targets):
+        parts = source.shape[0] if len(source.shape) != 2 else 2
+        rows = source.shape[0] // parts
+        for part in range(parts):
+            at = pl.ds(part * rows, rows)
+            copies.append(pltpu.make_async_copy(source.at[at], target.at[at], sem.at[len(copies)]))
+    for copy in copies:
+        copy.start()
+    for copy in copies:
+        copy.wait()
+
+
 def shards(tokens, cotangent, slot_rows, slot_count, slot_weight, w_in, w_out, momentum_in, momentum_out):
     any_ = pl.BlockSpec(memory_space=pl.ANY)
     vmem = pl.BlockSpec(memory_space=pltpu.VMEM)
     stages = STAGES_X + STAGES_G + STAGES_R
     grid5 = (4, 4, 2, CAP, D)
     mid = (2, 4, 4, 2, CAP, HALF)
+    blocks = (4, 4, 4, 2, CAP, QUARTER)
+    mid_blocks = (2, 2, 4, 4, 2, CAP, QUARTER)
     dma = pltpu.SemaphoreType.DMA
     outs = pl.pallas_call(
         kernel,
         out_shape=(
             pltpu.VMEM((256, D), BF16),
-            pltpu.VMEM((4, 4, 4, 2, CAP, QUARTER), BF16),
+            pltpu.VMEM(blocks, BF16),
             pltpu.VMEM((FF, D), BF16),
             pltpu.VMEM((2, QUARTER, FF), F32),
             pltpu.VMEM((FF, QUARTER), F32),
@@ -510,10 +518,10 @@
             pltpu.VMEM((ROWS, 256), BF16),
             pltpu.VMEM((ROWS, 128), F32),
             pltpu.VMEM(grid5, BF16),
-            pltpu.VMEM(grid5, BF16),
+            pltpu.VMEM(blocks, BF16),
             pltpu.VMEM(mid, BF16),
-            pltpu.VMEM(mid, BF16),
-            pltpu.VMEM(grid5, BF16),
+            pltpu.VMEM(mid_blocks, BF16),
+            pltpu.VMEM(blocks, BF16),
             pltpu.VMEM((2, D, FF), BF16),
             pltpu.VMEM((FF, D), BF16),
             pltpu.VMEM((ROWS, FF), F32),
@@ -531,9 +539,9 @@
             dma((stages, 2, 4)),
             dma((stages, 2)),
             dma((stages, 2)),
-            dma((3, STAGES_G, 2)),
-            dma((4, 4)),
-            dma((3, STAGES_G, 2)),
+            dma((2 + STAGES_G, 4)),
+            dma((2 + STAGES_G, 4)),
+            dma((2 + STAGES_G,)),
             dma((4,)),
             dma((4,)),
             dma((2, 6)),
@@ -549,6 +557,16 @@
         tokens[0], cotangent[0], slot_rows[0, 0], slot_count[0], slot_weight[0, 0],
         w_in[0], w_out[0], momentum_in[0], momentum_out[0],
     )
+    outs = [pltpu.with_memory_space_constraint(o, pltpu.VMEM) for o in outs]
+    outs = pl.pallas_call(
+        write_out,
+        out_shape=[pltpu.HBM(o.shape, o.dtype) for o in outs],
+        in_specs=[vmem] * 5,
+        out_specs=[pl.BlockSpec(memory_space=pltpu.HBM)] * 5,
+        scratch_shapes=[dma((16,))],
+        compiler_params=pltpu.CompilerParams(vmem_limit_bytes=1 << 20),
+        name="write_out",
+    )(*outs)
     outs = (outs[0], outs[1].reshape(2, D, FF)) + tuple(outs[2:])
     return tuple(o[None] for o in outs)
 

time: 227 us -> 221 us (0.974)
  local copies, waits for them, and re-layouts: 6.59 us -> 0 us
    unnamed x5 -> x0, local copies, waits for them, and re-layouts: 6.59 us -> none
    pallas_call x0 -> x1, Pallas kernels: none -> 4.05 us  [shards(): pl.pallas_call(write_out, out_shape=[pltpu.HBM(o.shape, o.dtype) for o in...]
    pallas_call x1, Pallas kernels: 220 us -> 216 us  [shards(): pl.pallas_call(kernel, out_shape=(pltpu.VMEM((256, D), BF16), pltpu.VMEM(...]
where the time goes in v2:
time: 221 us
  Pallas kernels  220 us (100%)
    pallas_call x1, Pallas kernels, shards(): pl.pallas_call(kernel, out_shape=(pltpu.VMEM((256, D), BF16), pltpu.VMEM(...  216 us

profile of v2, /device:TPU:0, one launch (start us, length us, event | category | flops | bytes accessed | tf_op | source)
XLA Modules:
  0.0 221.0 jit_solution(11694434422494286383)
XLA Ops:
  0.6 216.1 %step.1 = (bf16[256,2048]{1,0:T(8,128)(2,1)S(1)}, bf16[4,4,4,2,32,512]{5,4,3,2,1,0:T(8,128)(2,1)S(1)}, bf16[512,2048]{1,0:T(8,128)(2,1)S(1)}, f32[2,512,512]{2,1,0:T(8,128)S(1)}, f32[512,512]{1,0:T(8,128)S(1)}) custom-call(bf16[256,2048]{1,0:T(8,128)(2,1)} %bitcast.17, bf16[256,2048]{1,0:T(8,128)(2,1)} %bitcast.18, s32[32,32]{1,0:T(8,128)} %bitcast.20, ...), custom_call_target="tpu_custom_call" | custom-call | tf_op jit(solution)/shard_map/step/pallas_call | solution.py:505
  216.8 4.1 %write_out.1 = (bf16[256,2048]{1,0:T(8,128)(2,1)}, bf16[4,4,4,2,32,512]{5,4,3,2,1,0:T(8,128)(2,1)}, bf16[512,2048]{1,0:T(8,128)(2,1)}, f32[2,512,512]{2,1,0:T(8,128)}, f32[512,512]{1,0:T(8,128)}) custom-call(bf16[256,2048]{1,0:T(8,128)(2,1)S(1)} %get-tuple-element.15.refs_0_, bf16[4,4,4,2,32,512]{5,4,3,2,1,0:T(8,128)(2,1)S(1)} %get-tuple-element.16.refs_1_, ...), custom_call_target="tpu_custom_call" | custom-call | tf_op jit(solution)/shard_map/write_out/pallas_call | solution.py:561

commit v3 on v2

--- a/solution.py
+++ b/solution.py
@@ -32,8 +32,8 @@
     tok, xs, nwout, mom_in, mom_out,
     cot, onehot, scale, send_x, send_g, mid_x, mid_g, gs_, win, wout,
     act_a, act_s, hid, dh, dgu, grad_s, grad_r, gram,
-    load_sem, p1_send, p1_recv, p2_send, p2_recv, self1, self2,
-    rs_send, rs_recv, rs_self, gram_send, gram_recv, ag_send, ag_recv, fw_send, fw_recv,
+    load_sem, p1_send, p1_recv, p2_send, p2_recv,
+    rs_send, rs_recv, gram_sem, ag_send, ag_recv, ag_last, fw_sem,
 ):
     z = lax.axis_index("dp")
     e = lax.axis_index("expert")
@@ -121,26 +121,26 @@
         peer = expert_id(pa, y, pc) if half == 0 else expert_id(x, pa, pc)
         src, dst = first_views(send, mid, c0, w, half, pa, pc)
         return pltpu.make_async_remote_copy(
-            src_ref=src, dst_ref=dst, send_sem=p1_send.at[st, half, k], recv_sem=p1_recv.at[st, half, k],
+            src_ref=src, dst_ref=dst, send_sem=p1_send.at[st, half], recv_sem=p1_recv.at[st, half],
             device_id=(z, peer), device_id_type=MESH,
         )
 
     def p1_self(send, mid, st, c0, w, half):
         src, dst = first_views(send, mid, c0, w, half, x if half == 0 else y, c)
-        return pltpu.make_async_copy(src, dst, self1.at[st, half])
+        return pltpu.make_async_copy(src, dst, p1_recv.at[st, half])
 
     def p2_copy(mid, fin, st, c0, w, half, k):
         pa = lax.rem((y if half == 0 else x) + k, 4)
         peer = expert_id(x, pa, c) if half == 0 else expert_id(pa, y, c)
         src, dst = second_views(mid, fin, c0, w, half, pa)
         return pltpu.make_async_remote_copy(
-            src_ref=src, dst_ref=dst, send_sem=p2_send.at[st, half, k], recv_sem=p2_recv.at[st, half, k],
+            src_ref=src, dst_ref=dst, send_sem=p2_send.at[st, half], recv_sem=p2_recv.at[st, half],
             device_id=(z, peer), device_id_type=MESH,
         )
 
     def p2_self(mid, fin, st, c0, w, half):
         src, dst = second_views(mid, fin, c0, w, half, y if half == 0 else x)
-        return pltpu.make_async_copy(src, dst, self2.at[st, half])
+        return pltpu.make_async_copy(src, dst, p2_recv.at[st, half])
 
     def each(lo, hi, fn):
         def step(k, _):
@@ -149,6 +149,12 @@
 
         lax.fori_loop(lo, hi, step, 0)
 
+    def settle(view, sem):
+        pltpu.make_async_copy(view, view, sem).wait()
+
+    def share(w, blocks):
+        return hid.at[0 : blocks * 128, :] if w == QUARTER else onehot.at[0 : blocks * 128, :]
+
     def start_first(args):
         send, mid, fin, st, c0, w = args
 
@@ -163,16 +169,21 @@
     def forward(args):
         send, mid, fin, st, c0, w = args
         for half in range(2):
-            each(1, 8, lambda k: p1_copy(send, mid, st, c0, w, half, k).wait())
-            p1_self(send, mid, st, c0, w, half).wait()
+            landed = mid.at[half, :, :, :, :, :, pl.ds(c0, w)] if mid is mid_g else mid.at[half, :, :, :, :, pl.ds(c0, w)]
+            settle(landed, p1_recv.at[st, half])
+            settle(share(w, 7), p1_send.at[st, half])
             each(1, 4, lambda k: p2_copy(mid, fin, st, c0, w, half, k).start())
             p2_self(mid, fin, st, c0, w, half).start()
 
     def arrive(args):
         send, mid, fin, st, c0, w = args
         for half in range(2):
-            each(1, 4, lambda k: p2_copy(mid, fin, st, c0, w, half, k).wait())
-            p2_self(mid, fin, st, c0, w, half).wait()
+            if mid is mid_g:
+                landed = fin.at[pl.ds(2 * half, 2), :, :, :, :, pl.ds(c0, w)]
+            else:
+                landed = fin.at[2 * half + c0 // QUARTER]
+            settle(landed, p2_recv.at[st, half])
+            settle(share(w, 6), p2_send.at[st, half])
 
     wx, wg, wr = HALF // STAGES_X, QUARTER // STAGES_G, HALF // STAGES_R
     ex = [(send_x, mid_x, xs, s, s * wx, wx) for s in range(STAGES_X)]
@@ -194,9 +205,9 @@
         src = grad_s.at[2, q, :, pl.ds(s * wg, wg)]
         dst = grad_r.at[z, 2, :, pl.ds(s * wg, wg)]
         return pltpu.make_async_remote_copy(
-            src_ref=src, dst_ref=dst, send_sem=rs_send.at[2 + s, q],
-            recv_sem=rs_recv.at[2 + s, lax.rem(q - z + 4, 4)], device_id=(q, e), device_id_type=MESH,
-        ), pltpu.make_async_copy(src, dst, rs_self.at[2 + s])
+            src_ref=src, dst_ref=dst, send_sem=rs_send.at[2], recv_sem=rs_recv.at[2],
+            device_id=(q, e), device_id_type=MESH,
+        ), pltpu.make_async_copy(src, dst, rs_recv.at[2])
 
     def grad_out(s):
         cols = slice(s * wg, s * wg + wg)
@@ -239,12 +250,12 @@
         q = lax.rem(z + k, 4)
         return pltpu.make_async_remote_copy(
             src_ref=grad_s.at[mat, q], dst_ref=grad_r.at[z, mat],
-            send_sem=rs_send.at[mat, k], recv_sem=rs_recv.at[mat, k],
+            send_sem=rs_send.at[mat], recv_sem=rs_recv.at[mat],
             device_id=(q, e), device_id_type=MESH,
         )
 
     def in_self(mat):
-        return pltpu.make_async_copy(grad_s.at[mat, z], grad_r.at[z, mat], rs_self.at[mat])
+        return pltpu.make_async_copy(grad_s.at[mat, z], grad_r.at[z, mat], rs_recv.at[mat])
 
     def grad_in(mat):
         def step(j, _):
@@ -343,32 +354,14 @@
         start_first(er[s])
 
     sums = tuple(jnp.zeros((8, 128), F32) for _ in pairs)
-    for k in range(1, 4):
-        for j in range(STAGES_G):
-            pltpu.make_async_remote_copy(
-                src_ref=grad_s.at[2, 0, :, pl.ds(j * wg, wg)],
-                dst_ref=grad_r.at[lax.rem(z - k + 4, 4), 2, :, pl.ds(j * wg, wg)],
-                send_sem=rs_send.at[2 + j, k], recv_sem=rs_recv.at[2 + j, k],
-                device_id=(lax.rem(z + k, 4), e), device_id_type=MESH,
-            ).wait_recv()
-    for s in range(STAGES_G):
-        for q in range(4):
-            remote, local = out_copy(s, q)
-
-            @pl.when(z != q)
-            def _():
-                remote.wait_send()
-
-            @pl.when(z == q)
-            def _():
-                local.wait()
-
+    settle(grad_r.at[:, 2], rs_recv.at[2])
+    settle(grad_s.at[2, 0:3], rs_send.at[2])
     sums = gram_of(2, sums)
     for s in range(STAGES_R):
         forward(er[s])
     for mat in range(2):
-        each(1, 4, lambda k: in_copy(mat, k).wait())
-        in_self(mat).wait()
+        settle(grad_r.at[:, mat], rs_recv.at[mat])
+        settle(grad_s.at[mat, 0:3], rs_send.at[mat])
         sums = gram_of(mat, sums)
 
     own = jnp.concatenate([jnp.sum(t, axis=0, keepdims=True) for t in sums] + [jnp.zeros((6, 128), F32)], axis=0)
@@ -376,14 +369,15 @@
 
     def gram_copy(k):
         return pltpu.make_async_remote_copy(
-            src_ref=gram.at[z], dst_ref=gram.at[z], send_sem=gram_send.at[k], recv_sem=gram_recv.at[k],
+            src_ref=gram.at[z], dst_ref=gram.at[z], send_sem=gram_sem.at[0], recv_sem=gram_sem.at[1],
             device_id=(lax.rem(z + k, 4), e), device_id_type=MESH,
         )
 
     each(1, 4, lambda k: gram_copy(k).start())
     load[4].wait()
     load[5].wait()
-    each(1, 4, lambda k: gram_copy(k).wait())
+    settle(gram.at[0:3], gram_sem.at[1])
+    settle(gram.at[0:3], gram_sem.at[0])
     total = jnp.sum(gram[0] + gram[1] + gram[2] + gram[3], axis=1, keepdims=True)
     dots = {p: total[i : i + 1, :] for i, p in enumerate(pairs)}
 
@@ -409,7 +403,7 @@
     def ag_copy(mat, hh, direction):
         return pltpu.make_async_remote_copy(
             src_ref=slot(mat, hh, z), dst_ref=slot(mat, hh, z),
-            send_sem=ag_send.at[direction, 2 * mat + hh], recv_sem=ag_recv.at[direction, 2 * mat + hh],
+            send_sem=ag_send.at[0], recv_sem=ag_recv.at[2 * mat + hh] if direction == hh else ag_last.at[0],
             device_id=(lax.rem(z + (1 if direction == 0 else 3), 4), e), device_id_type=MESH,
         )
 
@@ -417,7 +411,7 @@
         owner = lax.rem(z + (3 if hh == 0 else 1), 4)
         return pltpu.make_async_remote_copy(
             src_ref=slot(mat, hh, owner), dst_ref=slot(mat, hh, owner),
-            send_sem=fw_send.at[2 * mat + hh], recv_sem=fw_recv.at[2 * mat + hh],
+            send_sem=fw_sem.at[0], recv_sem=fw_sem.at[1],
             device_id=(lax.rem(z + (1 if hh == 0 else 3), 4), e), device_id_type=MESH,
         )
 
@@ -470,12 +464,10 @@
     for mat in range(1, 3):
         for hh in range(2):
             pass_on(mat, hh)
-    for mat in range(3):
-        for hh in range(2):
-            ag_copy(mat, hh, 1 - hh).wait_recv()
-            ag_copy(mat, hh, 0).wait_send()
-            ag_copy(mat, hh, 1).wait_send()
-            fw_copy(mat, hh).wait()
+    settle(grad_s.at[0, 0:3], ag_last.at[0])
+    settle(grad_s.at[0:3, 0:2], ag_send.at[0])
+    settle(grad_s.at[0, 0:3], fw_sem.at[0])
+    settle(grad_s.at[0, 0:3], fw_sem.at[1])
 
 
 def write_out(*refs):
@@ -533,21 +525,17 @@
             pltpu.VMEM((4, 3, QUARTER, QUARTER), BF16),
             pltpu.VMEM((4, 16, 128), F32),
             dma((6,)),
-            dma((stages, 2, 8)),
-            dma((stages, 2, 8)),
-            dma((stages, 2, 4)),
-            dma((stages, 2, 4)),
             dma((stages, 2)),
             dma((stages, 2)),
-            dma((2 + STAGES_G, 4)),
-            dma((2 + STAGES_G, 4)),
-            dma((2 + STAGES_G,)),
-            dma((4,)),
-            dma((4,)),
-            dma((2, 6)),
-            dma((2, 6)),
+            dma((stages, 2)),
+            dma((stages, 2)),
+            dma((3,)),
+            dma((3,)),
+            dma((2,)),
+            dma((1,)),
             dma((6,)),
-            dma((6,)),
+            dma((1,)),
+            dma((2,)),
         ],
         compiler_params=pltpu.CompilerParams(
             collective_id=0, has_side_effects=True, vmem_limit_bytes=53 << 20

time: 221 us -> 217 us (0.982)
  Pallas kernels: 220 us -> 216 us
    pallas_call x1, Pallas kernels: 216 us -> 212 us  [shards(): pl.pallas_call(kernel, out_shape=(pltpu.VMEM((256, D), BF16), pltpu.VMEM(...]
where the time goes in v3:
time: 217 us
  Pallas kernels  216 us (100%)
    pallas_call x1, Pallas kernels, shards(): pl.pallas_call(kernel, out_shape=(pltpu.VMEM((256, D), BF16), pltpu.VMEM(...  212 us

profile of v3, /device:TPU:0, one launch (start us, length us, event | category | flops | bytes accessed | tf_op | source)
XLA Modules:
  0.0 217.0 jit_solution(6873775602289784082)
XLA Ops:
  0.6 212.3 %step.1 = (bf16[256,2048]{1,0:T(8,128)(2,1)S(1)}, bf16[4,4,4,2,32,512]{5,4,3,2,1,0:T(8,128)(2,1)S(1)}, bf16[512,2048]{1,0:T(8,128)(2,1)S(1)}, f32[2,512,512]{2,1,0:T(8,128)S(1)}, f32[512,512]{1,0:T(8,128)S(1)}) custom-call(bf16[256,2048]{1,0:T(8,128)(2,1)} %bitcast.17, bf16[256,2048]{1,0:T(8,128)(2,1)} %bitcast.18, s32[32,32]{1,0:T(8,128)} %bitcast.20, ...), custom_call_target="tpu_custom_call" | custom-call | tf_op jit(solution)/shard_map/step/pallas_call | solution.py:497
  212.9 4.1 %write_out.1 = (bf16[256,2048]{1,0:T(8,128)(2,1)}, bf16[4,4,4,2,32,512]{5,4,3,2,1,0:T(8,128)(2,1)}, bf16[512,2048]{1,0:T(8,128)(2,1)}, f32[2,512,512]{2,1,0:T(8,128)}, f32[512,512]{1,0:T(8,128)}) custom-call(bf16[256,2048]{1,0:T(8,128)(2,1)S(1)} %get-tuple-element.15.refs_0_, bf16[4,4,4,2,32,512]{5,4,3,2,1,0:T(8,128)(2,1)S(1)} %get-tuple-element.16.refs_1_, ...), custom_call_target="tpu_custom_call" | custom-call | tf_op jit(solution)/shard_map/write_out/pallas_call | solution.py:549

commit v4 on v3

--- a/solution.py
+++ b/solution.py
@@ -205,9 +205,9 @@
         src = grad_s.at[2, q, :, pl.ds(s * wg, wg)]
         dst = grad_r.at[z, 2, :, pl.ds(s * wg, wg)]
         return pltpu.make_async_remote_copy(
-            src_ref=src, dst_ref=dst, send_sem=rs_send.at[2], recv_sem=rs_recv.at[2],
+            src_ref=src, dst_ref=dst, send_sem=rs_send.at[2], recv_sem=rs_recv.at[4],
             device_id=(q, e), device_id_type=MESH,
-        ), pltpu.make_async_copy(src, dst, rs_recv.at[2])
+        ), pltpu.make_async_copy(src, dst, rs_recv.at[4])
 
     def grad_out(s):
         cols = slice(s * wg, s * wg + wg)
@@ -246,31 +246,35 @@
 
         lax.fori_loop(0, 4, step, 0)
 
-    def in_copy(mat, k):
+    def in_copy(mat, hh, k):
         q = lax.rem(z + k, 4)
-        return pltpu.make_async_remote_copy(
-            src_ref=grad_s.at[mat, q], dst_ref=grad_r.at[z, mat],
-            send_sem=rs_send.at[mat], recv_sem=rs_recv.at[mat],
+        part = pl.ds(hh * 256, 256)
+        return pltpu.make_async_remote_copy(
+            src_ref=grad_s.at[mat, q, part], dst_ref=grad_r.at[z, mat, part],
+            send_sem=rs_send.at[mat], recv_sem=rs_recv.at[2 * mat + hh],
             device_id=(q, e), device_id_type=MESH,
         )
 
-    def in_self(mat):
-        return pltpu.make_async_copy(grad_s.at[mat, z], grad_r.at[z, mat], rs_recv.at[mat])
-
-    def grad_in(mat):
+    def in_self(mat, hh):
+        part = pl.ds(hh * 256, 256)
+        return pltpu.make_async_copy(
+            grad_s.at[mat, z, part], grad_r.at[z, mat, part], rs_recv.at[2 * mat + hh]
+        )
+
+    def grad_in(mat, hh):
         def step(j, _):
-            k = lax.rem(2 + 3 * j, 4)
+            k = lax.rem(1 + 2 * j + j // 2, 4)
             q = lax.rem(z + k, 4)
-            rows = xs[q].reshape(ROWS, QUARTER)
-            grad_s[mat, q] = (dot(rows, dgu[mat], 0, 0) * scale_in).astype(BF16)
+            rows = xs[q, :, :, :, :, hh * 256 : hh * 256 + 256].reshape(ROWS, 256)
+            grad_s[mat, q, hh * 256 : hh * 256 + 256] = (dot(rows, dgu[mat], 0, 0) * scale_in).astype(BF16)
 
             @pl.when(k != 0)
             def _():
-                in_copy(mat, k).start()
+                in_copy(mat, hh, k).start()
 
             @pl.when(k == 0)
             def _():
-                in_self(mat).start()
+                in_self(mat, hh).start()
 
             return 0
 
@@ -298,13 +302,13 @@
                 total = part if total is None else total + part
         return total
 
-    def gram_of(mat, sums):
+    def gram_of(mat, hh, sums):
         def step(i, sums):
-            r = pl.ds(pl.multiple_of(i * 16, 16), 16)
+            r = pl.ds(pl.multiple_of(hh * 256 + i * 16, 16), 16)
             g = [grad_r[s, mat, r, :].astype(F32) for s in range(4)]
             return tuple(t + fold(g[a] * g[b]) for t, (a, b) in zip(sums, pairs))
 
-        return lax.fori_loop(0, 32, step, sums)
+        return lax.fori_loop(0, 16, step, sums)
 
     load[0].wait()
     gather(tok, send_x, ex[0][4], wx, False)
@@ -337,32 +341,34 @@
     arrive(eg[0])
     grad_out(0)
     hidden_grad(0)
+    forward(eg[3])
     arrive(eg[1])
     grad_out(1)
     hidden_grad(1)
-    forward(eg[3])
     arrive(eg[2])
     grad_out(2)
     hidden_grad(2)
     arrive(eg[3])
     grad_out(3)
     hidden_grad(3)
-    grad_in(0)
-    grad_in(1)
+    for mat in range(2):
+        for hh in range(2):
+            grad_in(mat, hh)
     for s in range(STAGES_R):
         rows_back(s)
         start_first(er[s])
 
     sums = tuple(jnp.zeros((8, 128), F32) for _ in pairs)
-    settle(grad_r.at[:, 2], rs_recv.at[2])
+    settle(grad_r.at[:, 2], rs_recv.at[4])
     settle(grad_s.at[2, 0:3], rs_send.at[2])
-    sums = gram_of(2, sums)
+    sums = gram_of(2, 1, gram_of(2, 0, sums))
     for s in range(STAGES_R):
         forward(er[s])
     for mat in range(2):
-        settle(grad_r.at[:, mat], rs_recv.at[mat])
+        for hh in range(2):
+            settle(grad_r.at[:, mat, pl.ds(hh * 256, 256)], rs_recv.at[2 * mat + hh])
+            sums = gram_of(mat, hh, sums)
         settle(grad_s.at[mat, 0:3], rs_send.at[mat])
-        sums = gram_of(mat, sums)
 
     own = jnp.concatenate([jnp.sum(t, axis=0, keepdims=True) for t in sums] + [jnp.zeros((6, 128), F32)], axis=0)
     gram[z] = own
@@ -530,7 +536,7 @@
             dma((stages, 2)),
             dma((stages, 2)),
             dma((3,)),
-            dma((3,)),
+            dma((5,)),
             dma((2,)),
             dma((1,)),
             dma((6,)),

time: 217 us -> 216 us (level)
  no operation moved by 1% of the time
where the time goes in v4:
time: 216 us
  Pallas kernels  215 us (100%)
    pallas_call x1, Pallas kernels, shards(): pl.pallas_call(kernel, out_shape=(pltpu.VMEM((256, D), BF16), pltpu.VMEM(...  211 us

profile of v4, /device:TPU:0, one launch (start us, length us, event | category | flops | bytes accessed | tf_op | source)
XLA Modules:
  0.0 216.3 jit_solution(14691599077385757257)
XLA Ops:
  0.6 211.4 %step.1 = (bf16[256,2048]{1,0:T(8,128)(2,1)S(1)}, bf16[4,4,4,2,32,512]{5,4,3,2,1,0:T(8,128)(2,1)S(1)}, bf16[512,2048]{1,0:T(8,128)(2,1)S(1)}, f32[2,512,512]{2,1,0:T(8,128)S(1)}, f32[512,512]{1,0:T(8,128)S(1)}) custom-call(bf16[256,2048]{1,0:T(8,128)(2,1)} %bitcast.17, bf16[256,2048]{1,0:T(8,128)(2,1)} %bitcast.18, s32[32,32]{1,0:T(8,128)} %bitcast.20, ...), custom_call_target="tpu_custom_call" | custom-call | tf_op jit(solution)/shard_map/step/pallas_call | solution.py:503
  212.1 4.1 %write_out.1 = (bf16[256,2048]{1,0:T(8,128)(2,1)}, bf16[4,4,4,2,32,512]{5,4,3,2,1,0:T(8,128)(2,1)}, bf16[512,2048]{1,0:T(8,128)(2,1)}, f32[2,512,512]{2,1,0:T(8,128)}, f32[512,512]{1,0:T(8,128)}) custom-call(bf16[256,2048]{1,0:T(8,128)(2,1)S(1)} %get-tuple-element.15.refs_0_, bf16[4,4,4,2,32,512]{5,4,3,2,1,0:T(8,128)(2,1)S(1)} %get-tuple-element.16.refs_1_, ...), custom_call_target="tpu_custom_call" | custom-call | tf_op jit(solution)/shard_map/write_out/pallas_call | solution.py:555

commit v5 on v4

--- a/solution.py
+++ b/solution.py
@@ -28,10 +28,10 @@
 
 
 def kernel(
-    tok_h, cot_h, rows_v, count_v, weight_v, win_h, wout_h, min_h, mout_h,
+    tok_h, cot_h, rows_h, count_h, weight_h, win_h, wout_h, min_h, mout_h,
     tok, xs, nwout, mom_in, mom_out,
     cot, onehot, scale, send_x, send_g, mid_x, mid_g, gs_, win, wout,
-    act_a, act_s, hid, dh, dgu, grad_s, grad_r, gram,
+    act_a, act_s, hid, dh, dgu, grad_s, grad_r, gram, rows_v, count_v, weight_v,
     load_sem, p1_send, p1_recv, p2_send, p2_recv,
     rs_send, rs_recv, gram_sem, ag_send, ag_recv, ag_last, fw_sem,
 ):
@@ -46,13 +46,6 @@
     def expert_id(px, py, pc):
         return (px * 4 + py) * 2 + pc
 
-    loads = [
-        (tok_h, tok), (cot_h, cot), (win_h, win), (wout_h, wout), (min_h, mom_in), (mout_h, mom_out),
-    ]
-    load = [pltpu.make_async_copy(s, d, load_sem.at[i]) for i, (s, d) in enumerate(loads)]
-    for copy in load[:2]:
-        copy.start()
-
     barrier = pltpu.get_barrier_semaphore()
 
     def greet(device):
@@ -64,6 +57,17 @@
         greet((z, expert_id(x, lax.rem(y + k // 2, 4), lax.rem(c + k % 2, 2))))
     for k in range(1, 4):
         greet((lax.rem(z + k, 4), e))
+
+    loads = [
+        (tok_h, tok), (cot_h, cot), (win_h, win), (wout_h, wout), (min_h, mom_in), (mout_h, mom_out),
+        (rows_h, rows_v), (count_h, count_v), (weight_h, weight_v),
+    ]
+    load = [pltpu.make_async_copy(s, d, load_sem.at[i]) for i, (s, d) in enumerate(loads)]
+    for copy in load[6:] + load[:2]:
+        copy.start()
+
+    for copy in load[6:]:
+        copy.wait()
 
     rows_t = jnp.transpose(rows_v[...])
     weight_t = jnp.transpose(weight_v[...])
@@ -308,13 +312,13 @@
             g = [grad_r[s, mat, r, :].astype(F32) for s in range(4)]
             return tuple(t + fold(g[a] * g[b]) for t, (a, b) in zip(sums, pairs))
 
-        return lax.fori_loop(0, 16, step, sums)
+        return lax.fori_loop(0, 16, step, sums, unroll=2)
 
     load[0].wait()
     gather(tok, send_x, ex[0][4], wx, False)
     pl.semaphore_wait(barrier, 16)
     start_first(ex[0])
-    for copy in load[2:]:
+    for copy in load[2:6]:
         copy.start()
     gather(tok, send_x, ex[1][4], wx, False)
     start_first(ex[1])
@@ -334,14 +338,15 @@
     arrive(ex[0])
     arrive(ex[1])
     start_first(eg[3])
-    each(0, 2, activate)
+    each(0, 1, activate)
     forward(eg[1])
-    each(2, 4, activate)
+    each(1, 3, activate)
     forward(eg[2])
+    each(3, 4, activate)
     arrive(eg[0])
     grad_out(0)
+    forward(eg[3])
     hidden_grad(0)
-    forward(eg[3])
     arrive(eg[1])
     grad_out(1)
     hidden_grad(1)
@@ -453,9 +458,6 @@
         ag_copy(mat, hh, hh).wait_recv()
         fw_copy(mat, hh).start()
 
-    pass_on(0, 0)
-    pass_on(0, 1)
-
     for s in range(STAGES_R):
         arrive(er[s])
 
@@ -466,6 +468,9 @@
         return 0
 
     lax.fori_loop(0, 4, tokens_step, 0)
+
+    pass_on(0, 0)
+    pass_on(0, 1)
 
     for mat in range(1, 3):
         for hh in range(2):
@@ -509,7 +514,7 @@
             pltpu.VMEM((2, QUARTER, FF), F32),
             pltpu.VMEM((FF, QUARTER), F32),
         ),
-        in_specs=[any_, any_, vmem, vmem, vmem, any_, any_, any_, any_],
+        in_specs=[any_] * 9,
         out_specs=(vmem,) * 5,
         scratch_shapes=[
             pltpu.VMEM((256, D), BF16),
@@ -530,7 +535,10 @@
             pltpu.VMEM((3, 4, QUARTER, QUARTER), BF16),
             pltpu.VMEM((4, 3, QUARTER, QUARTER), BF16),
             pltpu.VMEM((4, 16, 128), F32),
-            dma((6,)),
+            pltpu.VMEM((32, CAP), jnp.int32),
+            pltpu.VMEM((1, 32), jnp.int32),
+            pltpu.VMEM((32, CAP), F32),
+            dma((9,)),
             dma((stages, 2)),
             dma((stages, 2)),
             dma((stages, 2)),

time: 216 us -> 216 us (level)
  no operation moved by 1% of the time
where the time goes in v5:
time: 216 us
  Pallas kernels  215 us (100%)
    pallas_call x1, Pallas kernels, shards(): pl.pallas_call(kernel, out_shape=(pltpu.VMEM((256, D), BF16), pltpu.VMEM(...  211 us

profile of v5, /device:TPU:0, one launch (start us, length us, event | category | flops | bytes accessed | tf_op | source)
XLA Modules:
  0.0 215.6 jit_solution(6576419883993079217)
XLA Ops:
  0.6 210.7 %step.1 = (bf16[256,2048]{1,0:T(8,128)(2,1)S(1)}, bf16[4,4,4,2,32,512]{5,4,3,2,1,0:T(8,128)(2,1)S(1)}, bf16[512,2048]{1,0:T(8,128)(2,1)S(1)}, f32[2,512,512]{2,1,0:T(8,128)S(1)}, f32[512,512]{1,0:T(8,128)S(1)}) custom-call(bf16[256,2048]{1,0:T(8,128)(2,1)} %bitcast.17, bf16[256,2048]{1,0:T(8,128)(2,1)} %bitcast.18, s32[32,32]{1,0:T(8,128)} %bitcast.20, ...), custom_call_target="tpu_custom_call" | custom-call | tf_op jit(solution)/shard_map/step/pallas_call | solution.py:508
  211.4 4.1 %write_out.1 = (bf16[256,2048]{1,0:T(8,128)(2,1)}, bf16[4,4,4,2,32,512]{5,4,3,2,1,0:T(8,128)(2,1)}, bf16[512,2048]{1,0:T(8,128)(2,1)}, f32[2,512,512]{2,1,0:T(8,128)}, f32[512,512]{1,0:T(8,128)}) custom-call(bf16[256,2048]{1,0:T(8,128)(2,1)S(1)} %get-tuple-element.15.refs_0_, bf16[4,4,4,2,32,512]{5,4,3,2,1,0:T(8,128)(2,1)S(1)} %get-tuple-element.16.refs_1_, ...), custom_call_target="tpu_custom_call" | custom-call | tf_op jit(solution)/shard_map/write_out/pallas_call | solution.py:563

commit v6 on v5

--- a/solution.py
+++ b/solution.py
@@ -338,11 +338,10 @@
     arrive(ex[0])
     arrive(ex[1])
     start_first(eg[3])
-    each(0, 1, activate)
+    each(0, 2, activate)
     forward(eg[1])
-    each(1, 3, activate)
+    each(2, 4, activate)
     forward(eg[2])
-    each(3, 4, activate)
     arrive(eg[0])
     grad_out(0)
     forward(eg[3])

time: 216 us -> 216 us (level)
  no operation moved by 1% of the time
where the time goes in v6:
time: 216 us
  Pallas kernels  215 us (100%)
    pallas_call x1, Pallas kernels, shards(): pl.pallas_call(kernel, out_shape=(pltpu.VMEM((256, D), BF16), pltpu.VMEM(...  211 us

profile of v6, /device:TPU:0, one launch (start us, length us, event | category | flops | bytes accessed | tf_op | source)
XLA Modules:
  0.0 215.6 jit_solution(9174215366307228296)
XLA Ops:
  0.6 210.7 %step.1 = (bf16[256,2048]{1,0:T(8,128)(2,1)S(1)}, bf16[4,4,4,2,32,512]{5,4,3,2,1,0:T(8,128)(2,1)S(1)}, bf16[512,2048]{1,0:T(8,128)(2,1)S(1)}, f32[2,512,512]{2,1,0:T(8,128)S(1)}, f32[512,512]{1,0:T(8,128)S(1)}) custom-call(bf16[256,2048]{1,0:T(8,128)(2,1)} %bitcast.17, bf16[256,2048]{1,0:T(8,128)(2,1)} %bitcast.18, s32[32,32]{1,0:T(8,128)} %bitcast.20, ...), custom_call_target="tpu_custom_call" | custom-call | tf_op jit(solution)/shard_map/step/pallas_call | solution.py:507
  211.4 4.1 %write_out.1 = (bf16[256,2048]{1,0:T(8,128)(2,1)}, bf16[4,4,4,2,32,512]{5,4,3,2,1,0:T(8,128)(2,1)}, bf16[512,2048]{1,0:T(8,128)(2,1)}, f32[2,512,512]{2,1,0:T(8,128)}, f32[512,512]{1,0:T(8,128)}) custom-call(bf16[256,2048]{1,0:T(8,128)(2,1)S(1)} %get-tuple-element.15.refs_0_, bf16[4,4,4,2,32,512]{5,4,3,2,1,0:T(8,128)(2,1)S(1)} %get-tuple-element.16.refs_1_, ...), custom_call_target="tpu_custom_call" | custom-call | tf_op jit(solution)/shard_map/write_out/pallas_call | solution.py:562
